TPU v7x, 256 devices: a whole 4x4x8 slice. The times are simulated.
256 devices in a mesh: gx: 64 (over x, z, core), af: 4 (over y).
Axes of the slice: x: 4, y: 4, z: 8, core: 2. Of those that a mesh axis runs over, the one named last changes fastest.
Arguments:
- scalar_field: float32 [128, 512, 512], P('gx', 'af'), may hold values from -256 to 256
- plane_sketch: float32 [128, 2, 256], P('gx'), may hold values from -0.5 to 0.5
- second_sketch: float32 [512, 256], P('af'), may hold values from -0.25 to 0.25
- third_sketch: float32 [512, 256], replicated, may hold values from -0.25 to 0.25
- mixing: float32 [2, 256, 128], replicated, may hold values from -0.375 to 0.375
- plane_targets: int32 [128, 2], replicated, may hold values from 0 to 7
- plane_signs: int32 [128, 2], replicated, may hold values from 0 to 1
Outputs:
- factor_second: float32 [512, 128], P(('af', 'gx'))
- factor_third: float32 [512, 128], P(('gx', 'af'))
- core_sketch: float32 [128, 128, 128], P('gx', 'af')
Inputs may be any that keep to these rules, and one draw needn't show every extreme that they name: `plane_targets`: block id of each of a plane's two entries in the core sketch; the two may coincide. `plane_signs`: 1 stands for a plus sign, 0 for a minus sign.
All inputs are finite; a program needn't handle non-finite values.
Results may differ from a plain program's by a relative error of at most 0.0003.
Values sent between devices are 32-bit elements; how exact they have to be, the bound alone decides.
A program may use at most 64 MiB of HBM per device.

v0:
```python
import jax
import jax.numpy as jnp
from jax import lax
from jax.sharding import PartitionSpec as P

BLOCK = 16
BLOCKS = 8
precise = lax.Precision.HIGHEST


def gram_of(ranged):
    return jnp.dot(ranged.T, ranged, precision=precise)


def orthonormal_rows(ranged, gram_matrix):
    lower_factor = jnp.linalg.cholesky(gram_matrix)
    return jax.scipy.linalg.solve_triangular(lower_factor, ranged.T, lower=True).T


def selector(targets, sign_values, row_count):
    row_ids = jnp.arange(row_count, dtype=jnp.int32)
    return jnp.sum(
        jnp.where(targets[None, :, :] == row_ids[:, None, None], sign_values[None, :, :], 0.0),
        axis=2,
    )


def body(
    scalar_field, plane_sketch, second_sketch, third_sketch, mixing, plane_targets, plane_signs
):
    planes, rows, cells = scalar_field.shape
    rank_cols = mixing.shape[2]
    gx_index = lax.axis_index("gx")
    af_index = lax.axis_index("af")
    gx_size = lax.axis_size("gx")
    af_size = lax.axis_size("af")
    along_second = jnp.einsum("pjl,lk->pjk", scalar_field, third_sketch, precision=precise)
    partial_second = jnp.einsum(
        "pjk,pk->jk", along_second, plane_sketch[:, 0, :], precision=precise
    )
    along_third = jnp.einsum("pjl,jk->plk", scalar_field, second_sketch, precision=precise)
    partial_third = jnp.einsum("plk,pk->lk", along_third, plane_sketch[:, 1, :], precision=precise)
    range_second_block = jnp.dot(partial_second, mixing[0], precision=precise)
    range_third = jnp.dot(partial_third, mixing[1], precision=precise)
    full_rows = rows * af_size
    range_second = lax.dynamic_update_slice_in_dim(
        jnp.zeros((full_rows, rank_cols), jnp.float32), range_second_block, af_index * rows, 0
    )
    both = lax.psum(jnp.stack([range_second, range_third]), ("gx", "af"))
    rows_second, rows_third = (both[0], both[1])
    factor_second_all = orthonormal_rows(rows_second, gram_of(rows_second))
    factor_third_all = orthonormal_rows(rows_third, gram_of(rows_third))
    out_second = full_rows // (gx_size * af_size)
    factor_second = lax.dynamic_slice_in_dim(
        factor_second_all, (af_index * gx_size + gx_index) * out_second, out_second, 0
    )
    factor_third = lax.dynamic_slice_in_dim(
        factor_third_all, (gx_index * af_size + af_index) * out_second, out_second, 0
    )
    basis_second = lax.dynamic_slice_in_dim(factor_second_all, af_index * rows, rows, 0)
    left_side = jnp.einsum("jr,pjl->prl", basis_second, scalar_field, precision=precise)
    projected = jnp.einsum("prl,ls->prs", left_side, factor_third_all, precision=precise)
    out_rows = BLOCKS * BLOCK // gx_size
    plane_ids = jnp.arange(plane_targets.shape[0], dtype=jnp.int32)
    all_targets = plane_targets * BLOCK + (plane_ids % BLOCK)[:, None]
    all_signs = (2 * plane_signs - 1).astype(jnp.float32)
    first_plane = gx_index * planes
    own_targets = lax.dynamic_slice_in_dim(all_targets, first_plane, planes, 0)
    own_signs = lax.dynamic_slice_in_dim(all_signs, first_plane, planes, 0)
    flattened = projected.reshape(planes, -1)
    select = selector(own_targets, own_signs, gx_size * out_rows)
    partial_core = lax.psum_scatter(
        jnp.dot(select, flattened, precision=precise).reshape(
            gx_size * out_rows, rank_cols, rank_cols
        ),
        "gx",
        scatter_dimension=0,
        tiled=True,
    )
    core_sketch = lax.psum_scatter(partial_core, "af", scatter_dimension=1, tiled=True)
    return (factor_second, factor_third, core_sketch)


def solution(mesh):
    in_specs = (P("gx", "af", None), P("gx", None, None), P("af", None), P(), P(), P(), P())
    out_specs = (P(("af", "gx"), None), P(("gx", "af"), None), P("gx", "af", None))
    return jax.shard_map(body, mesh=mesh, in_specs=in_specs, out_specs=out_specs, check_vma=False)
```

profile of v0, /device:TPU:2, one launch (start us, length us, event | category | flops | bytes accessed | tf_op | source)
XLA Modules:
  0.0 544.3 jit_solution(9497696338969925887)
XLA Ops:
  7.2 0.0 all-reduce.4.cloned.1.call-start
  7.2 0.8 fusion.37
  8.0 0.2 copy-done
  8.2 2.0 fusion.1
  10.2 1.5 convolution_bitcast_fusion.2
  11.7 1.6 fusion.3
  13.4 1.2 fusion.4
  14.6 0.8 pad_maximum_fusion
  15.4 0.2 reduce-scatter.2.cloned.1.call-start
  15.7 0.7 add_convert_fusion
  16.4 0.7 multiply_add_fusion
  17.1 0.1 constant_dynamic-slice_fusion
  17.1 0.1 copy.38
  17.2 0.1 constant_dynamic-slice_fusion.1
  17.3 0.1 copy.37
  17.4 0.1 fusion.34
  17.5 253.1 %all-reduce.4.cloned.1.call-done = f32[2,512,128]{2,1,0:T(8,128)} async-done(((f32[2,512,128]{2,1,0:T(8,128)}), f32[2,512,128]{2,1,0:T(8,128)}) %all-reduce.4.cloned.1.call-update) | async-done | bytes 524304 | tf_op jit(solution)/shard_map/psum | solution.py:49
  270.6 1.6 fusion.13
  272.2 0.1 copy.35
  272.3 11.7 %cholesky.44 = f32[128,128]{1,0:T(8,128)S(1)} custom-call(f32[128,128]{1,0:T(8,128)S(1)} %fusion.32), custom_call_target="Cholesky" | custom-call | tf_op jit(solution)/shard_map/jit(cholesky)/cholesky | solution.py:16
  284.0 0.6 compare_reduce_fusion.1
  284.7 0.7 fusion.26
  285.4 9.8 %custom-call.6 = f32[1,128,128]{1,2,0:T(8,128)S(1)} custom-call(f32[1,128,128]{2,1,0:T(8,128)S(1)} %fusion.26), custom_call_target="InvertDiagBlocksLowerTriangular" | custom-call | tf_op jit(solution)/shard_map/jit(_solve_triangular)/triangular_solve | solution.py:17
  295.2 1.6 fusion.11
  296.8 0.1 copy.36
  296.9 11.7 %cholesky.55 = f32[128,128]{1,0:T(8,128)S(1)} custom-call(f32[128,128]{1,0:T(8,128)S(1)} %fusion.30), custom_call_target="Cholesky" | custom-call | tf_op jit(solution)/shard_map/jit(cholesky)/cholesky | solution.py:16
  308.7 0.6 compare_reduce_fusion
  309.3 0.7 fusion.27
  310.0 10.0 %custom-call.7 = f32[1,128,128]{1,2,0:T(8,128)S(1)} custom-call(f32[1,128,128]{2,1,0:T(8,128)S(1)} %fusion.27), custom_call_target="InvertDiagBlocksLowerTriangular" | custom-call | tf_op jit(solution)/shard_map/jit(_solve_triangular)/triangular_solve | solution.py:17
  320.0 1.4 fusion.8
  321.3 0.6 convolution_bitcast_fusion.1
  321.9 1.4 fusion.6
  323.3 0.6 convolution_bitcast_fusion.4
  323.9 6.8 %fusion.19 = f32[128,128,128]{2,0,1:T(8,128)S(1)} fusion(f32[1,2,128,128]{3,2,1,0:T(8,128)S(1)} %convolution_bitcast_fusion.4, f32[128,2]{0,1:T(2,128)S(1)} %fusion.34), kind=kOutput, calls=%fused_computation.27 | convolution fusion | flops 50331648 | bytes 8520704 | tf_op jit(solution)/shard_map/dot_general | solution.py:73
  330.7 8.3 %copy.39 = f32[128,128,128]{2,1,0:T(8,128)} copy(f32[128,128,128]{2,0,1:T(8,128)S(1)} %fusion.19) | data formatting | bytes 16777216 | tf_op jit(solution)/shard_map/dot_general | solution.py:73
  339.0 0.0 reduce-scatter.2.cloned.1.call-update
  339.0 0.0 all-reduce.6.cloned.1.call-start
  339.1 0.6 copy-done.1
  339.7 0.6 dynamic-slice.12
  340.9 147.6 %reduce-scatter.2.cloned.1.call-done = f32[2,128,128]{2,1,0:T(8,128)} async-done(((f32[128,128,128]{2,1,0:T(8,128)}), f32[2,128,128]{2,1,0:T(8,128)}) %reduce-scatter.2.cloned.1.call-update) | async-done | bytes 131088 | tf_op jit(solution)/shard_map/reduce_scatter | solution.py:72
  488.6 1.6 copy.40
  490.2 0.1 dynamic-slice_bitcast_fusion.1
  490.3 0.6 copy.41
  490.9 0.1 dynamic-slice_bitcast_fusion
  491.0 0.6 copy.42
  491.7 44.7 %all-reduce.6.cloned.1.call-done = f32[2,128,128]{2,0,1:T(2,128)} async-done(((f32[2,128,128]{2,0,1:T(2,128)}), f32[2,128,128]{2,0,1:T(2,128)}) %all-reduce.6.cloned.1.call-update) | async-done | bytes 131088
  536.4 0.8 constant_dynamic-slice_fusion.2
  537.1 0.6 copy.43
  (11 shorter events, 0.2 us)
Async XLA Ops:
  7.2 1.1 copy-start
  7.2 263.4 %all-reduce.4.cloned.1.call-start = ((), (), s32[]{:S(2)}) async-start(), calls=%async_computation.1 | async-start | bytes 1048576 | tf_op jit(solution)/shard_map/psum | solution.py:49
  15.4 473.1 %reduce-scatter.2.cloned.1.call-start = ((), (), s32[]{:S(2)}) async-start(), calls=%async_computation.2 | async-start | bytes 8519680 | tf_op jit(solution)/shard_map/reduce_scatter | solution.py:72
  339.0 0.7 copy-start.1
  339.0 197.4 %all-reduce.6.cloned.1.call-start = ((), (), s32[]{:S(2)}) async-start(), calls=%async_computation.3 | async-start | bytes 262144
Sparse Core Ops, SparseCore 0:
  15.6 254.9 all-reduce.3
  339.1 149.3 reduce-scatter.1
  491.0 45.3 all-reduce.5
where the time goes:
time: 545 us; the launch traced here: 544 us
  waiting for transfers between devices  445 us (82%)
  other arithmetic  48.2 us (9%)
  matrix products  20.2 us (4%)
  local copies, waits for them, and re-layouts  15.5 us (3%)
  between operations  14.6 us (3%)
    psum x1, waiting for transfers between devices, body(): both = lax.psum(jnp.stack([range_second, range_third]), ('gx', 'af'))  253 us
    reduce_scatter x1, waiting for transfers between devices, body(): lax.psum_scatter(jnp.dot(select, flattened, precision=precise).reshape(gx...  148 us
    unnamed x4, waiting for transfers between devices  44.8 us
    another operation x6, other arithmetic, orthonormal_rows(): lower_factor = jnp.linalg.cholesky(gram_matrix)  24.8 us
    another operation x4, other arithmetic, orthonormal_rows(): jax.scipy.linalg.solve_triangular(lower_factor, ranged.T, lower=True)  21.1 us
  transfers between devices with their start and end apart: 3, of which 3 were waited for; matrix products, arithmetic and copies ran while one was open for 1% of the time, Pallas kernels for 0%

commit v1 on v0

--- a/solution.py
+++ b/solution.py
@@ -46,7 +46,7 @@
     range_second = lax.dynamic_update_slice_in_dim(
         jnp.zeros((full_rows, rank_cols), jnp.float32), range_second_block, af_index * rows, 0
     )
-    both = lax.psum(jnp.stack([range_second, range_third]), ("gx", "af"))
+    both = lax.psum(lax.psum(jnp.stack([range_second, range_third]), "gx"), "af")
     rows_second, rows_third = (both[0], both[1])
     factor_second_all = orthonormal_rows(rows_second, gram_of(rows_second))
     factor_third_all = orthonormal_rows(rows_third, gram_of(rows_third))

time: 545 us -> 524 us (0.961)
  waiting for transfers between devices: 445 us -> 424 us
    psum x1 -> x2, waiting for transfers between devices: 253 us -> 230 us  [the longest x1 184 us: body(): lax.psum(jnp.stack([range_second, range_third]), 'gx')]
    unnamed x4 -> x5, waiting for transfers between devices: 44.8 us -> 44.7 us
  transfers between devices with their start and end apart: 3 -> 4, of which waited for: 3 -> 4; matrix products, arithmetic and copies ran while one was open for 1% -> 1% of each run, Pallas kernels for 0% -> 0%
where the time goes in v1:
time: 524 us; the launch traced here: 523 us
  waiting for transfers between devices  424 us (81%)
  other arithmetic  48.2 us (9%)
  matrix products  20.2 us (4%)
  local copies, waits for them, and re-layouts  15.5 us (3%)
  between operations  14.6 us (3%)
    psum x1, waiting for transfers between devices, body(): lax.psum(jnp.stack([range_second, range_third]), 'gx')  184 us
    reduce_scatter x1, waiting for transfers between devices, body(): lax.psum_scatter(jnp.dot(select, flattened, precision=precise).reshape(gx...  149 us
    psum x1, waiting for transfers between devices, body(): lax.psum(lax.psum(jnp.stack([range_second, range_third]), 'gx'), 'af')  46.8 us
    unnamed x5, waiting for transfers between devices  44.7 us
    another operation x6, other arithmetic, orthonormal_rows(): lower_factor = jnp.linalg.cholesky(gram_matrix)  24.8 us
    another operation x4, other arithmetic, orthonormal_rows(): jax.scipy.linalg.solve_triangular(lower_factor, ranged.T, lower=True)  21.1 us
  transfers between devices with their start and end apart: 4, of which 4 were waited for; matrix products, arithmetic and copies ran while one was open for 1% of the time, Pallas kernels for 0%

profile of v1, /device:TPU:2, one launch (start us, length us, event | category | flops | bytes accessed | tf_op | source)
XLA Modules:
  0.0 523.2 jit_solution(12720356529253345325)
XLA Ops:
  7.2 0.8 fusion.37
  8.0 0.2 copy-done
  8.2 2.0 fusion.1
  10.2 1.5 convolution_bitcast_fusion.2
  11.7 1.6 fusion.3
  13.4 1.2 fusion.4
  14.6 0.8 pad_maximum_fusion
  15.4 0.0 all-reduce.7.cloned.1.call-start
  15.5 0.7 add_convert_fusion
  16.2 0.1 constant_dynamic-slice_fusion
  16.3 0.1 copy.38
  16.4 183.5 %all-reduce.5.cloned.1.call-done = f32[2,512,128]{2,1,0:T(8,128)} async-done(((f32[2,512,128]{2,1,0:T(8,128)}), f32[2,512,128]{2,1,0:T(8,128)}) %all-reduce.5.cloned.1.call-update) | async-done | bytes 524304 | tf_op jit(solution)/shard_map/psum | solution.py:49
  199.9 0.2 reduce-scatter.2.cloned.1.call-start
  200.1 0.7 multiply_add_fusion
  200.8 0.1 constant_dynamic-slice_fusion.1
  200.9 0.1 copy.37
  201.0 0.1 fusion.34
  201.1 46.8 %all-reduce.7.cloned.1.call-done = f32[2,512,128]{2,1,0:T(8,128)} async-done(((f32[2,512,128]{2,1,0:T(8,128)}), f32[2,512,128]{2,1,0:T(8,128)}) %all-reduce.7.cloned.1.call-update) | async-done | bytes 524304 | tf_op jit(solution)/shard_map/psum | solution.py:49
  247.9 1.6 fusion.13
  249.5 0.1 copy.35
  249.6 11.7 %cholesky.44 = f32[128,128]{1,0:T(8,128)S(1)} custom-call(f32[128,128]{1,0:T(8,128)S(1)} %fusion.32), custom_call_target="Cholesky" | custom-call | tf_op jit(solution)/shard_map/jit(cholesky)/cholesky | solution.py:16
  261.4 0.6 compare_reduce_fusion.1
  262.0 0.7 fusion.26
  262.7 9.8 %custom-call.6 = f32[1,128,128]{1,2,0:T(8,128)S(1)} custom-call(f32[1,128,128]{2,1,0:T(8,128)S(1)} %fusion.26), custom_call_target="InvertDiagBlocksLowerTriangular" | custom-call | tf_op jit(solution)/shard_map/jit(_solve_triangular)/triangular_solve | solution.py:17
  272.5 1.6 fusion.11
  274.1 0.1 copy.36
  274.2 11.7 %cholesky.55 = f32[128,128]{1,0:T(8,128)S(1)} custom-call(f32[128,128]{1,0:T(8,128)S(1)} %fusion.30), custom_call_target="Cholesky" | custom-call | tf_op jit(solution)/shard_map/jit(cholesky)/cholesky | solution.py:16
  286.0 0.6 compare_reduce_fusion
  286.6 0.7 fusion.27
  287.3 10.0 %custom-call.7 = f32[1,128,128]{1,2,0:T(8,128)S(1)} custom-call(f32[1,128,128]{2,1,0:T(8,128)S(1)} %fusion.27), custom_call_target="InvertDiagBlocksLowerTriangular" | custom-call | tf_op jit(solution)/shard_map/jit(_solve_triangular)/triangular_solve | solution.py:17
  297.3 1.4 fusion.8
  298.7 0.6 convolution_bitcast_fusion.1
  299.3 1.4 fusion.6
  300.6 0.6 convolution_bitcast_fusion.4
  301.2 6.8 %fusion.19 = f32[128,128,128]{2,0,1:T(8,128)S(1)} fusion(f32[1,2,128,128]{3,2,1,0:T(8,128)S(1)} %convolution_bitcast_fusion.4, f32[128,2]{0,1:T(2,128)S(1)} %fusion.34), kind=kOutput, calls=%fused_computation.27 | convolution fusion | flops 50331648 | bytes 8520704 | tf_op jit(solution)/shard_map/dot_general | solution.py:73
  308.0 8.3 %copy.39 = f32[128,128,128]{2,1,0:T(8,128)} copy(f32[128,128,128]{2,0,1:T(8,128)S(1)} %fusion.19) | data formatting | bytes 16777216 | tf_op jit(solution)/shard_map/dot_general | solution.py:73
  316.4 0.0 all-reduce.9.cloned.1.call-start
  316.4 0.6 copy-done.1
  317.0 0.6 dynamic-slice.12
  318.2 149.3 %reduce-scatter.2.cloned.1.call-done = f32[2,128,128]{2,1,0:T(8,128)} async-done(((f32[128,128,128]{2,1,0:T(8,128)}), f32[2,128,128]{2,1,0:T(8,128)}) %reduce-scatter.2.cloned.1.call-update) | async-done | bytes 131088 | tf_op jit(solution)/shard_map/reduce_scatter | solution.py:72
  467.5 1.6 copy.40
  469.2 0.1 dynamic-slice_bitcast_fusion.1
  469.3 0.6 copy.41
  469.9 0.1 dynamic-slice_bitcast_fusion
  470.0 0.6 copy.42
  470.6 44.6 %all-reduce.9.cloned.1.call-done = f32[2,128,128]{2,0,1:T(2,128)} async-done(((f32[2,128,128]{2,0,1:T(2,128)}), f32[2,128,128]{2,0,1:T(2,128)}) %all-reduce.9.cloned.1.call-update) | async-done | bytes 131088
  515.2 0.8 constant_dynamic-slice_fusion.2
  516.0 0.6 copy.43
  (14 shorter events, 0.2 us)
Async XLA Ops:
  7.2 1.1 copy-start
  7.2 192.7 %all-reduce.5.cloned.1.call-start = ((), (), s32[]{:S(2)}) async-start(), calls=%async_computation.1 | async-start | bytes 1048576 | tf_op jit(solution)/shard_map/psum | solution.py:49
  15.4 232.5 %all-reduce.7.cloned.1.call-start = ((), (), s32[]{:S(2)}) async-start(), calls=%async_computation.2 | async-start | bytes 1048576 | tf_op jit(solution)/shard_map/psum | solution.py:49
  199.9 267.6 %reduce-scatter.2.cloned.1.call-start = ((), (), s32[]{:S(2)}) async-start(), calls=%async_computation.3 | async-start | bytes 8519680 | tf_op jit(solution)/shard_map/reduce_scatter | solution.py:72
  316.3 0.7 copy-start.1
  316.4 198.9 %all-reduce.9.cloned.1.call-start = ((), (), s32[]{:S(2)}) async-start(), calls=%async_computation.4 | async-start | bytes 262144
Sparse Core Ops, SparseCore 0:
  15.6 184.2 all-reduce.4
  202.2 45.6 all-reduce.6
  316.5 150.9 reduce-scatter.1
  469.8 45.4 all-reduce.8
